TPU v7x, 32 devices: a whole 2x2x4 slice. The times are simulated.
32 devices in a mesh: lon: 2 (over core), lat: 4 (over y, x), mem: 4 (over z).
Axes of the slice: x: 2, y: 2, z: 4, core: 2. Of those that a mesh axis runs over, the one named last changes fastest.
Arguments:
- ensemble: bfloat16 [80, 4, 4, 128, 512], P('mem', None, None, 'lon', 'lat'), may hold values from -6 to 6
- huber: float32 [4, 4, 128, 512], P(None, None, 'lon', 'lat'), may hold values from 0.1 to 1
- innovation: float32 [4, 4, 128, 512], P(None, None, 'lon', 'lat'), may hold values from -6 to 6
- sea_mask: int32 [32, 128], P('lon', 'lat'), may hold values 0 or 1
Outputs:
- control: float32 [80, 4, 32, 128], P('mem', None, 'lon', 'lat')
- gradient: float32 [80, 4, 32, 128], P('mem', None, 'lon', 'lat')
All inputs are finite; a program needn't handle non-finite values. No bound on the sum of `sea_mask` on one device may be relied on, other than what follows from the above.
Results may differ from a plain program's by a relative error of at most 0.013.
Values may be sent and summed in bfloat16 or wider, within the bound.
No kernel may reach another device: no remote copies, remote signals or barrier semaphores. Data moves between devices by JAX's collectives and lax.ppermute only.
A program may use at most 128 MiB of HBM per device.

v0:
```python
import math
import jax
import jax.numpy as jnp
from jax import lax
from jax.sharding import PartitionSpec as P

MEMBERS = 80
RATIO = 4
DSTEPS = 4
ITERS = 3
diffusion_rate = 0.2


def extended(cells, sides, width):
    for axis, dim in sides:
        count = lax.axis_size(axis)
        ends = count - 1
        head = lax.slice_in_dim(cells, 0, width, axis=dim)
        tail = lax.slice_in_dim(cells, cells.shape[dim] - width, cells.shape[dim], axis=dim)
        cells = jnp.concatenate(
            [
                lax.ppermute(tail, axis, [(i, (i + 1) % count) for i in range(ends)]),
                cells,
                lax.ppermute(head, axis, [((i + 1) % count, i) for i in range(ends)]),
            ],
            axis=dim,
        )
    return cells


def hat_table(rows, cols, row_shift, col_shift):
    fine_pos = (jnp.arange(rows, dtype=jnp.float32) - row_shift + 0.5) / RATIO - 0.5
    coarse_pos = jnp.arange(cols, dtype=jnp.float32) - col_shift
    return jnp.maximum(0.0, 1.0 - jnp.abs(coarse_pos[None, :] - fine_pos[:, None]))


def smooth_once(padded):
    inner = padded[:, :, 1:-1, 1:-1]
    beside = (
        padded[:, :, 2:, 1:-1]
        + padded[:, :, :-2, 1:-1]
        + padded[:, :, 1:-1, 2:]
        + padded[:, :, 1:-1, :-2]
    )
    return inner + diffusion_rate * (beside - 4.0 * inner)


def inside_cells(count, width, position, devices):
    first = position * count - width
    where = first + jnp.arange(count + 2 * width, dtype=jnp.int32)
    whole = count * devices
    return ((where >= 0) & (where < whole)).astype(jnp.float32)


def smooth_deep(field, width):
    padded = extended(field, (("lon", 2), ("lat", 3)), width)
    rows_in = inside_cells(field.shape[2], width, lax.axis_index("lon"), lax.axis_size("lon"))
    cols_in = inside_cells(field.shape[3], width, lax.axis_index("lat"), lax.axis_size("lat"))
    for step in range(DSTEPS):
        padded = smooth_once(padded)
        trim = step + 1
        row_keep = rows_in[trim : rows_in.shape[0] - trim]
        col_keep = cols_in[trim : cols_in.shape[0] - trim]
        padded = padded * row_keep[:, None] * col_keep[None, :]
    return padded


def local(ensemble, huber, innovation, sea_mask):
    scale = 1.0 / math.sqrt(MEMBERS - 1)
    keep = sea_mask.astype(jnp.float32)
    cells_x, cells_y = sea_mask.shape
    fine_cols, fine_rows = (ensemble.shape[3], ensemble.shape[4])
    forward_x = hat_table(fine_cols, cells_x + 2, 0, 1)
    forward_y = hat_table(fine_rows, cells_y + 2, 0, 1)
    back_x = hat_table(fine_cols + 4, cells_x, 2, 0)
    back_y = hat_table(fine_rows + 4, cells_y, 2, 0)

    def adjoint(misfit):
        spread = (
            jnp.einsum("mvlxy,vlxy->mlxy", ensemble, misfit, preferred_element_type=jnp.float32)
            * scale
        )
        padded = extended(spread, (("lon", 2), ("lat", 3)), 2)
        back = jnp.einsum(
            "xc,mlxy,yd->mlcd", back_x, padded, back_y, precision=lax.Precision.HIGHEST
        )
        back = smooth_deep(back, DSTEPS)
        return keep * back

    misfit_start = (huber * innovation).astype(jnp.bfloat16)
    gradient = -adjoint(misfit_start)
    control = jnp.zeros_like(gradient)
    for step in range(ITERS):
        shaped = keep * gradient
        hessian_padded = smooth_deep(shaped, DSTEPS + 1)
        fine = jnp.einsum(
            "xc,mlcd,yd->mlxy",
            forward_x,
            hessian_padded,
            forward_y,
            precision=lax.Precision.HIGHEST,
        ).astype(jnp.bfloat16)
        partial_sum = jnp.einsum(
            "mvlxy,mlxy->vlxy", ensemble, fine, preferred_element_type=jnp.float32
        )
        total = lax.psum(partial_sum, "mem")
        hessian_misfit = (huber * (total * scale)).astype(jnp.bfloat16)
        image = gradient + adjoint(hessian_misfit)
        squares, curvature = lax.psum(
            (jnp.sum(gradient * gradient), jnp.sum(gradient * image)), ("lon", "lat", "mem")
        )
        alpha = squares / curvature
        control = control - alpha * gradient
        gradient = gradient - alpha * image
    return (control, gradient)


def solution(mesh):
    placed = (
        P("mem", None, None, "lon", "lat"),
        P(None, None, "lon", "lat"),
        P(None, None, "lon", "lat"),
        P("lon", "lat"),
    )
    return jax.shard_map(
        local,
        mesh=mesh,
        in_specs=placed,
        out_specs=(P("mem", None, "lon", "lat"), P("mem", None, "lon", "lat")),
        check_vma=False,
    )
```

profile of v0, /device:TPU:0, one launch (start us, length us, event | category | flops | bytes accessed | tf_op | source)
XLA Modules:
  0.0 666.2 jit_solution(17996090135539417670)
XLA Ops:
  8.5 4.2 fusion.3
  21.2 4.0 fusion.330
  31.3 5.4 collective-permute-start.2
  40.5 11.1 %fusion.7 = f32[20,4,132,16]{2,3,1,0:T(8,128)S(1)} fusion(f32[20,4,68,2]{2,3,1,0:T(2,128)S(1)} %copy.100, f32[20,4,68,128]{2,3,1,0:T(8,128)} %copy.99, f32[20,4,68,2]{2,3,1,0:T(2,128)S(1)} %copy.98, f32[68]{0:T(128)S(1)} %multiply_add_fusion.3), kind=kOutput, calls=%fused_computation.14 | convolution fusion | flops 139311872 | bytes 3548432 | tf_op jit(solution)/shard_map/xc,mlxy,yd->mlcd/dot_general | solution.py:84
  59.0 4.5 collective-permute-start.6
  67.9 4.4 collective-permute-done.7
  87.9 4.2 collective-permute-start.10
  97.8 4.5 collective-permute-done.11
  117.4 37.6 %all-reduce.7.cloned.1.call-done = f32[4,4,64,128]{3,2,1,0:T(8,128)} async-done(((f32[4,4,64,128]{3,2,1,0:T(8,128)}), f32[4,4,64,128]{3,2,1,0:T(8,128)}) %all-reduce.7.cloned.1.call-update) | async-done | bytes 524304 | tf_op jit(solution)/shard_map/psum | solution.py:106
  156.1 4.2 fusion.4
  167.7 4.0 fusion.329
  174.1 4.0 collective-permute-start.14
  188.7 11.1 %fusion.13 = f32[20,4,132,16]{2,3,1,0:T(8,128)S(1)} fusion(f32[20,4,68,2]{2,3,1,0:T(2,128)S(1)} %copy.115, f32[20,4,68,128]{2,3,1,0:T(8,128)} %copy.114, f32[20,4,68,2]{2,3,1,0:T(2,128)S(1)} %copy.113, f32[68]{0:T(128)} %copy-done.22), kind=kOutput, calls=%fused_computation.20 | convolution fusion | flops 139311872 | bytes 3548432 | tf_op jit(solution)/shard_map/xc,mlxy,yd->mlcd/dot_general | solution.py:84
  208.1 4.1 collective-permute-start.18
  216.8 5.2 collective-permute-done.19
  229.8 39.9 %all-reduce.2 = (f32[]{:T(128)}, f32[]{:T(128)}) all-reduce(f32[]{:T(128)} %get-tuple-element.7, f32[]{:T(128)} %get-tuple-element.6), channel_id=1, replica_groups=mesh['lon'=2,'lat'=4,'mem'=4] {'lon','lat','mem'}, use_global_device_ids=true, to_apply=%region_1.0 | all-reduce | flops 2 | bytes 16 | tf_op jit(solution)/shard_map/psum | solution.py:109
  281.3 4.9 collective-permute-start.22
  292.0 4.9 collective-permute-done.23
  311.9 37.1 %all-reduce.9.cloned.1.call-done = f32[4,4,64,128]{3,2,1,0:T(8,128)} async-done(((f32[4,4,64,128]{3,2,1,0:T(8,128)}), f32[4,4,64,128]{3,2,1,0:T(8,128)}) %all-reduce.9.cloned.1.call-update) | async-done | bytes 524304 | tf_op jit(solution)/shard_map/psum | solution.py:106
  350.1 4.2 fusion.5
  368.0 4.0 collective-permute-start.26
  382.7 11.1 %fusion.19 = f32[20,4,132,16]{2,3,1,0:T(8,128)S(1)} fusion(f32[20,4,68,2]{2,3,1,0:T(2,128)S(1)} %copy.130, f32[20,4,68,128]{2,3,1,0:T(8,128)} %copy.129, f32[20,4,68,2]{2,3,1,0:T(2,128)S(1)} %copy.128, f32[68]{0:T(128)} %copy-done.22), kind=kOutput, calls=%fused_computation.26 | convolution fusion | flops 139311872 | bytes 3548432 | tf_op jit(solution)/shard_map/xc,mlxy,yd->mlcd/dot_general | solution.py:84
  410.6 5.1 collective-permute-done.31
  423.6 39.5 %all-reduce.1 = (f32[]{:T(128)}, f32[]{:T(128)}) all-reduce(f32[]{:T(128)} %get-tuple-element.5, f32[]{:T(128)} %get-tuple-element.4), channel_id=1, replica_groups=mesh['lon'=2,'lat'=4,'mem'=4] {'lon','lat','mem'}, use_global_device_ids=true, to_apply=%region_6.0 | all-reduce | flops 2 | bytes 16 | tf_op jit(solution)/shard_map/psum | solution.py:109
  474.7 4.9 collective-permute-start.34
  485.4 5.0 collective-permute-done.35
  505.1 37.3 %all-reduce.11.cloned.1.call-done = f32[4,4,64,128]{3,2,1,0:T(8,128)} async-done(((f32[4,4,64,128]{3,2,1,0:T(8,128)}), f32[4,4,64,128]{3,2,1,0:T(8,128)}) %all-reduce.11.cloned.1.call-update) | async-done | bytes 524304 | tf_op jit(solution)/shard_map/psum | solution.py:106
  543.6 4.2 fusion.6
  561.7 4.0 collective-permute-start.38
  576.3 11.1 %fusion.25 = f32[20,4,132,16]{2,3,1,0:T(8,128)S(1)} fusion(f32[20,4,68,2]{2,3,1,0:T(2,128)S(1)} %copy.145, f32[20,4,68,128]{2,3,1,0:T(8,128)} %copy.144, f32[20,4,68,2]{2,3,1,0:T(2,128)S(1)} %copy.143, f32[68]{0:T(128)} %copy-done.22), kind=kOutput, calls=%fused_computation.32 | convolution fusion | flops 139311872 | bytes 3548432 | tf_op jit(solution)/shard_map/xc,mlxy,yd->mlcd/dot_general | solution.py:84
  604.3 5.2 collective-permute-done.43
  617.3 39.5 %all-reduce = (f32[]{:T(128)}, f32[]{:T(128)}) all-reduce(f32[]{:T(128)} %get-tuple-element.3, f32[]{:T(128)} %get-tuple-element.2), channel_id=1, replica_groups=mesh['lon'=2,'lat'=4,'mem'=4] {'lon','lat','mem'}, use_global_device_ids=true, to_apply=%region_11.0 | all-reduce | flops 2 | bytes 16 | tf_op jit(solution)/shard_map/psum | solution.py:109
  (377 shorter events, 271.5 us)
Async XLA Ops:
  7.2 147.8 %all-reduce.7.cloned.1.call-start = ((), (), s32[]{:S(2)}) async-start(), calls=%async_computation | async-start | bytes 1048576 | tf_op jit(solution)/shard_map/psum | solution.py:106
  15.0 3.8 collective-permute-start
  27.6 12.7 %collective-permute-start.3 = (f32[20,4,68,2]{2,1,3,0:T(4,128)S(1)}, f32[20,4,68,2]{2,1,3,0:T(4,128)S(1)}, u32[]{:S(2)}, u32[]{:S(2)}) collective-permute-start(f32[20,4,68,2]{2,1,3,0:T(4,128)S(1)} %copy.214), channel_id=1, source_target_pairs={{4,0},{8,4},{12,8},{5,1},{9,5},{13,9},{6,2},{10,6},{14,10},{7,3},{... | collective-permute-start | bytes 130568 | tf_op jit(solution)/shard_map/ppermute | solution.py:24
  31.3 9.1 %collective-permute-start.2 = (f32[20,4,68,2]{2,1,3,0:T(4,128)S(1)}, f32[20,4,68,2]{2,1,3,0:T(4,128)S(1)}, u32[]{:S(2)}, u32[]{:S(2)}) collective-permute-start(f32[20,4,68,2]{2,1,3,0:T(4,128)S(1)} %copy.213), channel_id=1, source_target_pairs={{0,4},{4,8},{8,12},{1,5},{5,9},{9,13},{2,6},{6,10},{10,14},{3,7},{... | collective-permute-start | bytes 130568 | tf_op jit(solution)/shard_map/ppermute | solution.py:22
  54.7 3.3 collective-permute-start.5
  59.0 8.3 %collective-permute-start.6 = (f32[20,4,24,4]{2,3,1,0:T(4,128)S(1)}, f32[20,4,24,4]{2,3,1,0:T(4,128)S(1)}, u32[]{:S(2)}, u32[]{:S(2)}) collective-permute-start(f32[20,4,24,4]{2,3,1,0:T(4,128)S(1)} %copy.101), channel_id=1, source_target_pairs={{0,4},{4,8},{8,12},{1,5},{5,9},{9,13},{2,6},{6,10},{10,14},{3,7},{... | collective-permute-start | bytes 92168 | tf_op jit(solution)/shard_map/ppermute | solution.py:22
  64.2 8.1 %collective-permute-start.7 = (f32[20,4,24,4]{2,3,1,0:T(4,128)S(1)}, f32[20,4,24,4]{2,3,1,0:T(4,128)}, u32[]{:S(2)}, u32[]{:S(2)}) collective-permute-start(f32[20,4,24,4]{2,3,1,0:T(4,128)S(1)} %copy.102), channel_id=1, source_target_pairs={{4,0},{8,4},{12,8},{5,1},{9,5},{13,9},{6,2},{10,6},{14,10},{7,3},{... | collective-permute-start | bytes 92168 | tf_op jit(solution)/shard_map/ppermute | solution.py:24
  80.0 3.5 collective-permute-start.9
  87.9 8.4 %collective-permute-start.10 = (f32[20,4,26,5]{2,1,3,0:T(4,128)}, f32[20,4,26,5]{2,1,3,0:T(4,128)}, u32[]{:S(2)}, u32[]{:S(2)}) collective-permute-start(f32[20,4,26,5]{2,1,3,0:T(4,128)} %copy.105), channel_id=1, source_target_pairs={{0,4},{4,8},{8,12},{1,5},{5,9},{9,13},{2,6},{6,10},{10,14},{3,7},{... | collective-permute-start | bytes 124808 | tf_op jit(solution)/shard_map/ppermute | solution.py:22
  93.3 9.0 %collective-permute-start.11 = (f32[20,4,26,5]{2,1,3,0:T(4,128)}, f32[20,4,26,5]{2,1,3,0:T(4,128)}, u32[]{:S(2)}, u32[]{:S(2)}) collective-permute-start(f32[20,4,26,5]{2,1,3,0:T(4,128)} %copy.106), channel_id=1, source_target_pairs={{4,0},{8,4},{12,8},{5,1},{9,5},{13,9},{6,2},{10,6},{14,10},{7,3},{... | collective-permute-start | bytes 124808 | tf_op jit(solution)/shard_map/ppermute | solution.py:24
  117.0 232.0 %all-reduce.9.cloned.1.call-start = ((), (), s32[]{:S(2)}) async-start(), calls=%async_computation.1 | async-start | bytes 1048576 | tf_op jit(solution)/shard_map/psum | solution.py:106
  174.1 12.1 %collective-permute-start.14 = (f32[20,4,68,2]{2,1,3,0:T(4,128)S(1)}, f32[20,4,68,2]{2,1,3,0:T(4,128)}, u32[]{:S(2)}, u32[]{:S(2)}) collective-permute-start(f32[20,4,68,2]{2,1,3,0:T(4,128)S(1)} %copy.215), channel_id=1, source_target_pairs={{0,4},{4,8},{8,12},{1,5},{5,9},{9,13},{2,6},{6,10},{10,14},{3,7},{... | collective-permute-start | bytes 130568 | tf_op jit(solution)/shard_map/ppermute | solution.py:22
  181.1 6.6 collective-permute-start.15
  202.4 3.3 collective-permute-start.17
  208.1 8.2 %collective-permute-start.18 = (f32[20,4,24,4]{2,3,1,0:T(4,128)}, f32[20,4,24,4]{2,3,1,0:T(4,128)S(1)}, u32[]{:S(2)}, u32[]{:S(2)}) collective-permute-start(f32[20,4,24,4]{2,3,1,0:T(4,128)} %copy.116), channel_id=1, source_target_pairs={{0,4},{4,8},{8,12},{1,5},{5,9},{9,13},{2,6},{6,10},{10,14},{3,7},{... | collective-permute-start | bytes 92168 | tf_op jit(solution)/shard_map/ppermute | solution.py:22
  212.8 9.2 %collective-permute-start.19 = (f32[20,4,24,4]{2,3,1,0:T(4,128)S(1)}, f32[20,4,24,4]{2,3,1,0:T(4,128)}, u32[]{:S(2)}, u32[]{:S(2)}) collective-permute-start(f32[20,4,24,4]{2,3,1,0:T(4,128)S(1)} %copy.117), channel_id=1, source_target_pairs={{4,0},{8,4},{12,8},{5,1},{9,5},{13,9},{6,2},{10,6},{14,10},{7,3},{... | collective-permute-start | bytes 92168 | tf_op jit(solution)/shard_map/ppermute | solution.py:24
  273.4 3.5 collective-permute-start.21
  281.3 9.1 %collective-permute-start.22 = (f32[20,4,26,5]{2,1,3,0:T(4,128)}, f32[20,4,26,5]{2,1,3,0:T(4,128)}, u32[]{:S(2)}, u32[]{:S(2)}) collective-permute-start(f32[20,4,26,5]{2,1,3,0:T(4,128)} %copy.120), channel_id=1, source_target_pairs={{0,4},{4,8},{8,12},{1,5},{5,9},{9,13},{2,6},{6,10},{10,14},{3,7},{... | collective-permute-start | bytes 124808 | tf_op jit(solution)/shard_map/ppermute | solution.py:22
  287.5 9.5 %collective-permute-start.23 = (f32[20,4,26,5]{2,1,3,0:T(4,128)}, f32[20,4,26,5]{2,1,3,0:T(4,128)}, u32[]{:S(2)}, u32[]{:S(2)}) collective-permute-start(f32[20,4,26,5]{2,1,3,0:T(4,128)} %copy.121), channel_id=1, source_target_pairs={{4,0},{8,4},{12,8},{5,1},{9,5},{13,9},{6,2},{10,6},{14,10},{7,3},{... | collective-permute-start | bytes 124808 | tf_op jit(solution)/shard_map/ppermute | solution.py:24
  311.6 230.8 %all-reduce.11.cloned.1.call-start = ((), (), s32[]{:S(2)}) async-start(), calls=%async_computation.2 | async-start | bytes 1048576 | tf_op jit(solution)/shard_map/psum | solution.py:106
  368.0 11.9 %collective-permute-start.26 = (f32[20,4,68,2]{2,1,3,0:T(4,128)S(1)}, f32[20,4,68,2]{2,1,3,0:T(4,128)}, u32[]{:S(2)}, u32[]{:S(2)}) collective-permute-start(f32[20,4,68,2]{2,1,3,0:T(4,128)S(1)} %copy.217), channel_id=1, source_target_pairs={{0,4},{4,8},{8,12},{1,5},{5,9},{9,13},{2,6},{6,10},{10,14},{3,7},{... | collective-permute-start | bytes 130568 | tf_op jit(solution)/shard_map/ppermute | solution.py:22
  375.1 6.6 collective-permute-start.27
  396.4 3.3 collective-permute-start.29
  402.0 8.0 %collective-permute-start.30 = (f32[20,4,24,4]{2,3,1,0:T(4,128)}, f32[20,4,24,4]{2,3,1,0:T(4,128)S(1)}, u32[]{:S(2)}, u32[]{:S(2)}) collective-permute-start(f32[20,4,24,4]{2,3,1,0:T(4,128)} %copy.131), channel_id=1, source_target_pairs={{0,4},{4,8},{8,12},{1,5},{5,9},{9,13},{2,6},{6,10},{10,14},{3,7},{... | collective-permute-start | bytes 92168 | tf_op jit(solution)/shard_map/ppermute | solution.py:22
  406.6 9.2 %collective-permute-start.31 = (f32[20,4,24,4]{2,3,1,0:T(4,128)S(1)}, f32[20,4,24,4]{2,3,1,0:T(4,128)}, u32[]{:S(2)}, u32[]{:S(2)}) collective-permute-start(f32[20,4,24,4]{2,3,1,0:T(4,128)S(1)} %copy.132), channel_id=1, source_target_pairs={{4,0},{8,4},{12,8},{5,1},{9,5},{13,9},{6,2},{10,6},{14,10},{7,3},{... | collective-permute-start | bytes 92168 | tf_op jit(solution)/shard_map/ppermute | solution.py:24
  466.8 3.5 collective-permute-start.33
  474.7 9.1 %collective-permute-start.34 = (f32[20,4,26,5]{2,1,3,0:T(4,128)}, f32[20,4,26,5]{2,1,3,0:T(4,128)}, u32[]{:S(2)}, u32[]{:S(2)}) collective-permute-start(f32[20,4,26,5]{2,1,3,0:T(4,128)} %copy.135), channel_id=1, source_target_pairs={{0,4},{4,8},{8,12},{1,5},{5,9},{9,13},{2,6},{6,10},{10,14},{3,7},{... | collective-permute-start | bytes 124808 | tf_op jit(solution)/shard_map/ppermute | solution.py:22
  480.9 9.5 %collective-permute-start.35 = (f32[20,4,26,5]{2,1,3,0:T(4,128)}, f32[20,4,26,5]{2,1,3,0:T(4,128)}, u32[]{:S(2)}, u32[]{:S(2)}) collective-permute-start(f32[20,4,26,5]{2,1,3,0:T(4,128)} %copy.136), channel_id=1, source_target_pairs={{4,0},{8,4},{12,8},{5,1},{9,5},{13,9},{6,2},{10,6},{14,10},{7,3},{... | collective-permute-start | bytes 124808 | tf_op jit(solution)/shard_map/ppermute | solution.py:24
  561.7 12.0 %collective-permute-start.38 = (f32[20,4,68,2]{2,1,3,0:T(4,128)S(1)}, f32[20,4,68,2]{2,1,3,0:T(4,128)}, u32[]{:S(2)}, u32[]{:S(2)}) collective-permute-start(f32[20,4,68,2]{2,1,3,0:T(4,128)S(1)} %copy.219), channel_id=1, source_target_pairs={{0,4},{4,8},{8,12},{1,5},{5,9},{9,13},{2,6},{6,10},{10,14},{3,7},{... | collective-permute-start | bytes 130568 | tf_op jit(solution)/shard_map/ppermute | solution.py:22
  568.8 6.6 collective-permute-start.39
  595.7 8.0 %collective-permute-start.42 = (f32[20,4,24,4]{2,3,1,0:T(4,128)}, f32[20,4,24,4]{2,3,1,0:T(4,128)S(1)}, u32[]{:S(2)}, u32[]{:S(2)}) collective-permute-start(f32[20,4,24,4]{2,3,1,0:T(4,128)} %copy.146), channel_id=1, source_target_pairs={{0,4},{4,8},{8,12},{1,5},{5,9},{9,13},{2,6},{6,10},{10,14},{3,7},{... | collective-permute-start | bytes 92168 | tf_op jit(solution)/shard_map/ppermute | solution.py:22
  600.2 9.2 %collective-permute-start.43 = (f32[20,4,24,4]{2,3,1,0:T(4,128)S(1)}, f32[20,4,24,4]{2,3,1,0:T(4,128)}, u32[]{:S(2)}, u32[]{:S(2)}) collective-permute-start(f32[20,4,24,4]{2,3,1,0:T(4,128)S(1)} %copy.147), channel_id=1, source_target_pairs={{4,0},{8,4},{12,8},{5,1},{9,5},{13,9},{6,2},{10,6},{14,10},{7,3},{... | collective-permute-start | bytes 92168 | tf_op jit(solution)/shard_map/ppermute | solution.py:24
  (80 other events, 843.9 us)
Sparse Core Ops, SparseCore 0:
  117.1 37.8 all-reduce.6
  311.8 37.1 all-reduce.8
  505.3 37.1 all-reduce.10
where the time goes:
time: 674 us; the launch traced here: 666 us
  waiting for transfers between devices  182 us (27%)
  blocking collectives  119 us (18%)
  local copies, waits for them, and re-layouts  113 us (17%)
  starting transfers between devices  94.1 us (14%)
  other arithmetic  76.6 us (11%)
  matrix products  61.5 us (9%)
  between operations  20 us (3%)
    psum x3, blocking collectives, local(): lax.psum((jnp.sum(gradient * gradient), jnp.sum(gradient * image)), ('lon...  119 us
    psum x3, waiting for transfers between devices, local(): total = lax.psum(partial_sum, 'mem')  112 us
    ppermute x22, starting transfers between devices, extended(): lax.ppermute(tail, axis, [(i, (i + 1) % count) for i in range(ends)])  63.9 us
    ppermute x22, waiting for transfers between devices, extended(): lax.ppermute(head, axis, [((i + 1) % count, i) for i in range(ends)])  58.4 us
    dot_general x8, matrix products, adjoint(): jnp.einsum('xc,mlxy,yd->mlcd', back_x, padded, back_y, precision=lax.Prec...  49.3 us
    slice x29, local copies, waits for them, and re-layouts, extended(): lax.slice_in_dim(cells, cells.shape[dim] - width, cells.shape[dim], axis=...  34.3 us
    unnamed x142, local copies, waits for them, and re-layouts  31.1 us
    ppermute x22, starting transfers between devices, extended(): lax.ppermute(head, axis, [((i + 1) % count, i) for i in range(ends)])  29.5 us
  transfers between devices with their start and end apart: 47, of which 31 were waited for; matrix products, arithmetic and copies ran while one was open for 6% of the time, Pallas kernels for 0%

commit v1 on v0

--- a/solution.py
+++ b/solution.py
@@ -103,7 +103,7 @@
         partial_sum = jnp.einsum(
             "mvlxy,mlxy->vlxy", ensemble, fine, preferred_element_type=jnp.float32
         )
-        total = lax.psum(partial_sum, "mem")
+        total = jnp.sum(lax.all_gather(partial_sum, "mem"), axis=0)
         hessian_misfit = (huber * (total * scale)).astype(jnp.bfloat16)
         image = gradient + adjoint(hessian_misfit)
         squares, curvature = lax.psum(

time: 674 us -> 696 us (1.033)
  waiting for transfers between devices: 182 us -> 205 us
    all_gather x0 -> x3, waiting for transfers between devices: none -> 134 us  [local(): total = jnp.sum(lax.all_gather(partial_sum, 'mem'), axis=0)]
    psum x3 -> x0, waiting for transfers between devices: 112 us -> none  [local(): total = lax.psum(partial_sum, 'mem')]
  transfers between devices with their start and end apart: 47 -> 47, of which waited for: 31 -> 32; matrix products, arithmetic and copies ran while one was open for 6% -> 6% of each run, Pallas kernels for 0% -> 0%
where the time goes in v1:
time: 696 us; the launch traced here: 688 us
  waiting for transfers between devices  205 us (29%)
  blocking collectives  115 us (17%)
  local copies, waits for them, and re-layouts  113 us (16%)
  starting transfers between devices  94.2 us (14%)
  other arithmetic  78.9 us (11%)
  matrix products  61.5 us (9%)
  between operations  20 us (3%)
    all_gather x3, waiting for transfers between devices, local(): total = jnp.sum(lax.all_gather(partial_sum, 'mem'), axis=0)  134 us
    psum x3, blocking collectives, local(): lax.psum((jnp.sum(gradient * gradient), jnp.sum(gradient * image)), ('lon...  115 us
    ppermute x22, starting transfers between devices, extended(): lax.ppermute(tail, axis, [(i, (i + 1) % count) for i in range(ends)])  63.2 us
    ppermute x22, waiting for transfers between devices, extended(): lax.ppermute(head, axis, [((i + 1) % count, i) for i in range(ends)])  60.2 us
    dot_general x8, matrix products, adjoint(): jnp.einsum('xc,mlxy,yd->mlcd', back_x, padded, back_y, precision=lax.Prec...  49.3 us
    slice x29, local copies, waits for them, and re-layouts, extended(): lax.slice_in_dim(cells, cells.shape[dim] - width, cells.shape[dim], axis=...  34.3 us
    unnamed x142, local copies, waits for them, and re-layouts  31.1 us
    ppermute x22, starting transfers between devices, extended(): lax.ppermute(head, axis, [((i + 1) % count, i) for i in range(ends)])  30 us
  transfers between devices with their start and end apart: 47, of which 32 were waited for; matrix products, arithmetic and copies ran while one was open for 6% of the time, Pallas kernels for 0%

profile of v1, /device:TPU:0, one launch (start us, length us, event | category | flops | bytes accessed | tf_op | source)
XLA Modules:
  0.0 688.4 jit_solution(11107706044351017210)
XLA Ops:
  8.5 4.2 fusion.3
  21.2 4.0 fusion.330
  27.6 4.2 collective-permute-start.2
  40.7 11.1 %fusion.7 = f32[20,4,132,16]{2,3,1,0:T(8,128)S(1)} fusion(f32[20,4,68,2]{2,3,1,0:T(2,128)S(1)} %copy.110, f32[20,4,68,128]{2,3,1,0:T(8,128)} %copy.109, f32[20,4,68,2]{2,3,1,0:T(2,128)S(1)} %copy.108, f32[68]{0:T(128)S(1)} %multiply_add_fusion.3), kind=kOutput, calls=%fused_computation.14 | convolution fusion | flops 139311872 | bytes 3548432 | tf_op jit(solution)/shard_map/xc,mlxy,yd->mlcd/dot_general | solution.py:84
  58.7 4.3 collective-permute-start.6
  67.3 5.6 collective-permute-done.7
  88.5 4.2 collective-permute-start.10
  98.5 4.5 collective-permute-done.11
  118.0 44.7 %all-gather.7.cloned.1.call-done = f32[16,4,64,128]{3,2,1,0:T(8,128)} async-done(((f32[4,4,64,128]{3,2,1,0:T(8,128)}), f32[16,4,64,128]{3,2,1,0:T(8,128)}) %all-gather.7.cloned.1.call-update) | async-done | bytes 2097168 | tf_op jit(solution)/shard_map/all_gather | solution.py:106
  164.6 4.2 fusion.4
  182.9 4.0 collective-permute-start.14
  197.5 11.1 %fusion.13 = f32[20,4,132,16]{2,3,1,0:T(8,128)S(1)} fusion(f32[20,4,68,2]{2,3,1,0:T(2,128)S(1)} %copy.125, f32[20,4,68,128]{2,3,1,0:T(8,128)} %copy.124, f32[20,4,68,2]{2,3,1,0:T(2,128)S(1)} %copy.123, f32[68]{0:T(128)} %copy-done.22), kind=kOutput, calls=%fused_computation.20 | convolution fusion | flops 139311872 | bytes 3548432 | tf_op jit(solution)/shard_map/xc,mlxy,yd->mlcd/dot_general | solution.py:84
  216.9 4.1 collective-permute-start.18
  225.6 5.1 collective-permute-done.19
  238.6 38.5 %all-reduce.2 = (f32[]{:T(128)}, f32[]{:T(128)}) all-reduce(f32[]{:T(128)} %get-tuple-element.7, f32[]{:T(128)} %get-tuple-element.6), channel_id=1, replica_groups=mesh['lon'=2,'lat'=4,'mem'=4] {'lon','lat','mem'}, use_global_device_ids=true, to_apply=%region_1.0 | all-reduce | flops 2 | bytes 16 | tf_op jit(solution)/shard_map/psum | solution.py:109
  288.7 4.9 collective-permute-start.22
  299.4 4.9 collective-permute-done.23
  319.5 44.3 %all-gather.9.cloned.1.call-done = f32[16,4,64,128]{3,2,1,0:T(8,128)} async-done(((f32[4,4,64,128]{3,2,1,0:T(8,128)}), f32[16,4,64,128]{3,2,1,0:T(8,128)}) %all-gather.9.cloned.1.call-update) | async-done | bytes 2097168 | tf_op jit(solution)/shard_map/all_gather | solution.py:106
  365.7 4.2 fusion.5
  383.9 4.0 collective-permute-start.26
  398.5 11.1 %fusion.19 = f32[20,4,132,16]{2,3,1,0:T(8,128)S(1)} fusion(f32[20,4,68,2]{2,3,1,0:T(2,128)S(1)} %copy.140, f32[20,4,68,128]{2,3,1,0:T(8,128)} %copy.139, f32[20,4,68,2]{2,3,1,0:T(2,128)S(1)} %copy.138, f32[68]{0:T(128)} %copy-done.22), kind=kOutput, calls=%fused_computation.26 | convolution fusion | flops 139311872 | bytes 3548432 | tf_op jit(solution)/shard_map/xc,mlxy,yd->mlcd/dot_general | solution.py:84
  417.9 4.1 collective-permute-start.30
  426.7 5.2 collective-permute-done.31
  439.6 38.3 %all-reduce.1 = (f32[]{:T(128)}, f32[]{:T(128)}) all-reduce(f32[]{:T(128)} %get-tuple-element.5, f32[]{:T(128)} %get-tuple-element.4), channel_id=1, replica_groups=mesh['lon'=2,'lat'=4,'mem'=4] {'lon','lat','mem'}, use_global_device_ids=true, to_apply=%region_6.0 | all-reduce | flops 2 | bytes 16 | tf_op jit(solution)/shard_map/psum | solution.py:109
  489.6 4.9 collective-permute-start.34
  500.3 5.0 collective-permute-done.35
  520.0 44.7 %all-gather.11.cloned.1.call-done = f32[16,4,64,128]{3,2,1,0:T(8,128)} async-done(((f32[4,4,64,128]{3,2,1,0:T(8,128)}), f32[16,4,64,128]{3,2,1,0:T(8,128)}) %all-gather.11.cloned.1.call-update) | async-done | bytes 2097168 | tf_op jit(solution)/shard_map/all_gather | solution.py:106
  566.6 4.4 fusion.6
  599.6 11.1 %fusion.25 = f32[20,4,132,16]{2,3,1,0:T(8,128)S(1)} fusion(f32[20,4,68,2]{2,3,1,0:T(2,128)S(1)} %copy.155, f32[20,4,68,128]{2,3,1,0:T(8,128)} %copy.154, f32[20,4,68,2]{2,3,1,0:T(2,128)S(1)} %copy.153, f32[68]{0:T(128)} %copy-done.22), kind=kOutput, calls=%fused_computation.32 | convolution fusion | flops 139311872 | bytes 3548432 | tf_op jit(solution)/shard_map/xc,mlxy,yd->mlcd/dot_general | solution.py:84
  619.0 4.2 collective-permute-start.42
  627.6 5.2 collective-permute-done.43
  640.6 38.3 %all-reduce = (f32[]{:T(128)}, f32[]{:T(128)}) all-reduce(f32[]{:T(128)} %get-tuple-element.3, f32[]{:T(128)} %get-tuple-element.2), channel_id=1, replica_groups=mesh['lon'=2,'lat'=4,'mem'=4] {'lon','lat','mem'}, use_global_device_ids=true, to_apply=%region_11.0 | all-reduce | flops 2 | bytes 16 | tf_op jit(solution)/shard_map/psum | solution.py:109
  (380 shorter events, 275.4 us)
Async XLA Ops:
  7.2 155.6 %all-gather.7.cloned.1.call-start = ((), (), s32[]{:S(2)}) async-start(), calls=%async_computation | async-start | bytes 2621440 | tf_op jit(solution)/shard_map/all_gather | solution.py:106
  15.0 3.8 collective-permute-start
  27.6 12.1 %collective-permute-start.2 = (f32[20,4,68,2]{2,1,3,0:T(4,128)S(1)}, f32[20,4,68,2]{2,1,3,0:T(4,128)S(1)}, u32[]{:S(2)}, u32[]{:S(2)}) collective-permute-start(f32[20,4,68,2]{2,1,3,0:T(4,128)S(1)} %copy.223), channel_id=1, source_target_pairs={{0,4},{4,8},{8,12},{1,5},{5,9},{9,13},{2,6},{6,10},{10,14},{3,7},{... | collective-permute-start | bytes 130568 | tf_op jit(solution)/shard_map/ppermute | solution.py:22
  34.3 6.3 collective-permute-start.3
  58.7 8.1 %collective-permute-start.6 = (f32[20,4,24,4]{2,3,1,0:T(4,128)S(1)}, f32[20,4,24,4]{2,3,1,0:T(4,128)S(1)}, u32[]{:S(2)}, u32[]{:S(2)}) collective-permute-start(f32[20,4,24,4]{2,3,1,0:T(4,128)S(1)} %copy.111), channel_id=1, source_target_pairs={{0,4},{4,8},{8,12},{1,5},{5,9},{9,13},{2,6},{6,10},{10,14},{3,7},{... | collective-permute-start | bytes 92168 | tf_op jit(solution)/shard_map/ppermute | solution.py:22
  63.6 9.3 %collective-permute-start.7 = (f32[20,4,24,4]{2,3,1,0:T(4,128)S(1)}, f32[20,4,24,4]{2,3,1,0:T(4,128)}, u32[]{:S(2)}, u32[]{:S(2)}) collective-permute-start(f32[20,4,24,4]{2,3,1,0:T(4,128)S(1)} %copy.112), channel_id=1, source_target_pairs={{4,0},{8,4},{12,8},{5,1},{9,5},{13,9},{6,2},{10,6},{14,10},{7,3},{... | collective-permute-start | bytes 92168 | tf_op jit(solution)/shard_map/ppermute | solution.py:24
  80.6 3.5 collective-permute-start.9
  88.5 8.4 %collective-permute-start.10 = (f32[20,4,26,5]{2,1,3,0:T(4,128)}, f32[20,4,26,5]{2,1,3,0:T(4,128)}, u32[]{:S(2)}, u32[]{:S(2)}) collective-permute-start(f32[20,4,26,5]{2,1,3,0:T(4,128)} %copy.115), channel_id=1, source_target_pairs={{0,4},{4,8},{8,12},{1,5},{5,9},{9,13},{2,6},{6,10},{10,14},{3,7},{... | collective-permute-start | bytes 124808 | tf_op jit(solution)/shard_map/ppermute | solution.py:22
  93.9 9.0 %collective-permute-start.11 = (f32[20,4,26,5]{2,1,3,0:T(4,128)}, f32[20,4,26,5]{2,1,3,0:T(4,128)}, u32[]{:S(2)}, u32[]{:S(2)}) collective-permute-start(f32[20,4,26,5]{2,1,3,0:T(4,128)} %copy.116), channel_id=1, source_target_pairs={{4,0},{8,4},{12,8},{5,1},{9,5},{13,9},{6,2},{10,6},{14,10},{7,3},{... | collective-permute-start | bytes 124808 | tf_op jit(solution)/shard_map/ppermute | solution.py:24
  117.6 246.2 %all-gather.9.cloned.1.call-start = ((), (), s32[]{:S(2)}) async-start(), calls=%async_computation.1 | async-start | bytes 2621440 | tf_op jit(solution)/shard_map/all_gather | solution.py:106
  182.9 12.1 %collective-permute-start.14 = (f32[20,4,68,2]{2,1,3,0:T(4,128)S(1)}, f32[20,4,68,2]{2,1,3,0:T(4,128)}, u32[]{:S(2)}, u32[]{:S(2)}) collective-permute-start(f32[20,4,68,2]{2,1,3,0:T(4,128)S(1)} %copy.225), channel_id=1, source_target_pairs={{0,4},{4,8},{8,12},{1,5},{5,9},{9,13},{2,6},{6,10},{10,14},{3,7},{... | collective-permute-start | bytes 130568 | tf_op jit(solution)/shard_map/ppermute | solution.py:22
  189.9 6.6 collective-permute-start.15
  211.2 3.3 collective-permute-start.17
  216.9 8.2 %collective-permute-start.18 = (f32[20,4,24,4]{2,3,1,0:T(4,128)}, f32[20,4,24,4]{2,3,1,0:T(4,128)S(1)}, u32[]{:S(2)}, u32[]{:S(2)}) collective-permute-start(f32[20,4,24,4]{2,3,1,0:T(4,128)} %copy.126), channel_id=1, source_target_pairs={{0,4},{4,8},{8,12},{1,5},{5,9},{9,13},{2,6},{6,10},{10,14},{3,7},{... | collective-permute-start | bytes 92168 | tf_op jit(solution)/shard_map/ppermute | solution.py:22
  221.6 9.2 %collective-permute-start.19 = (f32[20,4,24,4]{2,3,1,0:T(4,128)S(1)}, f32[20,4,24,4]{2,3,1,0:T(4,128)}, u32[]{:S(2)}, u32[]{:S(2)}) collective-permute-start(f32[20,4,24,4]{2,3,1,0:T(4,128)S(1)} %copy.127), channel_id=1, source_target_pairs={{4,0},{8,4},{12,8},{5,1},{9,5},{13,9},{6,2},{10,6},{14,10},{7,3},{... | collective-permute-start | bytes 92168 | tf_op jit(solution)/shard_map/ppermute | solution.py:24
  280.8 3.5 collective-permute-start.21
  288.7 9.1 %collective-permute-start.22 = (f32[20,4,26,5]{2,1,3,0:T(4,128)}, f32[20,4,26,5]{2,1,3,0:T(4,128)}, u32[]{:S(2)}, u32[]{:S(2)}) collective-permute-start(f32[20,4,26,5]{2,1,3,0:T(4,128)} %copy.130), channel_id=1, source_target_pairs={{0,4},{4,8},{8,12},{1,5},{5,9},{9,13},{2,6},{6,10},{10,14},{3,7},{... | collective-permute-start | bytes 124808 | tf_op jit(solution)/shard_map/ppermute | solution.py:22
  294.9 9.5 %collective-permute-start.23 = (f32[20,4,26,5]{2,1,3,0:T(4,128)}, f32[20,4,26,5]{2,1,3,0:T(4,128)}, u32[]{:S(2)}, u32[]{:S(2)}) collective-permute-start(f32[20,4,26,5]{2,1,3,0:T(4,128)} %copy.131), channel_id=1, source_target_pairs={{4,0},{8,4},{12,8},{5,1},{9,5},{13,9},{6,2},{10,6},{14,10},{7,3},{... | collective-permute-start | bytes 124808 | tf_op jit(solution)/shard_map/ppermute | solution.py:24
  319.0 245.7 %all-gather.11.cloned.1.call-start = ((), (), s32[]{:S(2)}) async-start(), calls=%async_computation.2 | async-start | bytes 2621440 | tf_op jit(solution)/shard_map/all_gather | solution.py:106
  383.9 12.1 %collective-permute-start.26 = (f32[20,4,68,2]{2,1,3,0:T(4,128)S(1)}, f32[20,4,68,2]{2,1,3,0:T(4,128)}, u32[]{:S(2)}, u32[]{:S(2)}) collective-permute-start(f32[20,4,68,2]{2,1,3,0:T(4,128)S(1)} %copy.227), channel_id=1, source_target_pairs={{0,4},{4,8},{8,12},{1,5},{5,9},{9,13},{2,6},{6,10},{10,14},{3,7},{... | collective-permute-start | bytes 130568 | tf_op jit(solution)/shard_map/ppermute | solution.py:22
  390.9 6.6 collective-permute-start.27
  412.2 3.3 collective-permute-start.29
  417.9 8.2 %collective-permute-start.30 = (f32[20,4,24,4]{2,3,1,0:T(4,128)}, f32[20,4,24,4]{2,3,1,0:T(4,128)S(1)}, u32[]{:S(2)}, u32[]{:S(2)}) collective-permute-start(f32[20,4,24,4]{2,3,1,0:T(4,128)} %copy.141), channel_id=1, source_target_pairs={{0,4},{4,8},{8,12},{1,5},{5,9},{9,13},{2,6},{6,10},{10,14},{3,7},{... | collective-permute-start | bytes 92168 | tf_op jit(solution)/shard_map/ppermute | solution.py:22
  422.6 9.2 %collective-permute-start.31 = (f32[20,4,24,4]{2,3,1,0:T(4,128)S(1)}, f32[20,4,24,4]{2,3,1,0:T(4,128)}, u32[]{:S(2)}, u32[]{:S(2)}) collective-permute-start(f32[20,4,24,4]{2,3,1,0:T(4,128)S(1)} %copy.142), channel_id=1, source_target_pairs={{4,0},{8,4},{12,8},{5,1},{9,5},{13,9},{6,2},{10,6},{14,10},{7,3},{... | collective-permute-start | bytes 92168 | tf_op jit(solution)/shard_map/ppermute | solution.py:24
  481.7 3.5 collective-permute-start.33
  489.6 9.1 %collective-permute-start.34 = (f32[20,4,26,5]{2,1,3,0:T(4,128)}, f32[20,4,26,5]{2,1,3,0:T(4,128)}, u32[]{:S(2)}, u32[]{:S(2)}) collective-permute-start(f32[20,4,26,5]{2,1,3,0:T(4,128)} %copy.145), channel_id=1, source_target_pairs={{0,4},{4,8},{8,12},{1,5},{5,9},{9,13},{2,6},{6,10},{10,14},{3,7},{... | collective-permute-start | bytes 124808 | tf_op jit(solution)/shard_map/ppermute | solution.py:22
  495.7 9.5 %collective-permute-start.35 = (f32[20,4,26,5]{2,1,3,0:T(4,128)}, f32[20,4,26,5]{2,1,3,0:T(4,128)}, u32[]{:S(2)}, u32[]{:S(2)}) collective-permute-start(f32[20,4,26,5]{2,1,3,0:T(4,128)} %copy.146), channel_id=1, source_target_pairs={{4,0},{8,4},{12,8},{5,1},{9,5},{13,9},{6,2},{10,6},{14,10},{7,3},{... | collective-permute-start | bytes 124808 | tf_op jit(solution)/shard_map/ppermute | solution.py:24
  585.0 12.0 %collective-permute-start.38 = (f32[20,4,68,2]{2,1,3,0:T(4,128)S(1)}, f32[20,4,68,2]{2,1,3,0:T(4,128)}, u32[]{:S(2)}, u32[]{:S(2)}) collective-permute-start(f32[20,4,68,2]{2,1,3,0:T(4,128)S(1)} %copy.229), channel_id=1, source_target_pairs={{0,4},{4,8},{8,12},{1,5},{5,9},{9,13},{2,6},{6,10},{10,14},{3,7},{... | collective-permute-start | bytes 130568 | tf_op jit(solution)/shard_map/ppermute | solution.py:22
  592.1 6.6 collective-permute-start.39
  613.3 3.3 collective-permute-start.41
  619.0 8.0 %collective-permute-start.42 = (f32[20,4,24,4]{2,3,1,0:T(4,128)}, f32[20,4,24,4]{2,3,1,0:T(4,128)S(1)}, u32[]{:S(2)}, u32[]{:S(2)}) collective-permute-start(f32[20,4,24,4]{2,3,1,0:T(4,128)} %copy.156), channel_id=1, source_target_pairs={{0,4},{4,8},{8,12},{1,5},{5,9},{9,13},{2,6},{6,10},{10,14},{3,7},{... | collective-permute-start | bytes 92168 | tf_op jit(solution)/shard_map/ppermute | solution.py:22
  623.7 9.0 %collective-permute-start.43 = (f32[20,4,24,4]{2,3,1,0:T(4,128)S(1)}, f32[20,4,24,4]{2,3,1,0:T(4,128)}, u32[]{:S(2)}, u32[]{:S(2)}) collective-permute-start(f32[20,4,24,4]{2,3,1,0:T(4,128)S(1)} %copy.157), channel_id=1, source_target_pairs={{4,0},{8,4},{12,8},{5,1},{9,5},{13,9},{6,2},{10,6},{14,10},{7,3},{... | collective-permute-start | bytes 92168 | tf_op jit(solution)/shard_map/ppermute | solution.py:24
  (80 other events, 870.5 us)
Sparse Core Ops, SparseCore 0:
  117.7 45.0 all-gather.6
  319.2 44.5 all-gather.8
  520.1 44.5 all-gather.10
